TPU v7x, 256 devices: a whole 4x4x8 slice. The times are simulated.
256 devices in a mesh: seq: 8 (over x, y_hi), dp: 32 (over y_lo, z, core).
Axes of the slice: x: 4, y: 4 (y_hi: 2, y_lo: 2; y = y_hi * 2 + y_lo), z: 8, core: 2. Of those that a mesh axis runs over, the one named last changes fastest.
Arguments:
- frames: bfloat16 [64, 1024, 3072], P('dp', 'seq'), may hold values from -6 to 6
- proj_weight: bfloat16 [3072, 4608], P('dp'), may hold values from -0.109375 to 0.109375
- rate_weight: bfloat16 [3072, 24], replicated, may hold values from -0.109375 to 0.109375
- rate_bias: float32 [24], replicated, may hold values from -2 to 1
- init_weights: float32 [2, 24, 64, 256], replicated, may hold values from -0.75 to 0.75
- init_bias_hidden: float32 [24, 256], replicated, may hold values from -3 to 3
- init_bias_out: float32 [24, 64], replicated, may hold values from -3 to 3
- out_gain: float32 [1536], replicated, may hold values from 0.5 to 1.5
Outputs:
- ttt_output: bfloat16 [64, 1024, 1536], P('dp', 'seq')
All inputs are finite; a program needn't handle non-finite values.
Results may differ from a plain program's by a relative error of at most 0.0091.
Values may be sent and summed in bfloat16 or wider, within the bound.
No kernel may reach another device: no remote copies, remote signals or barrier semaphores. Data moves between devices by JAX's collectives and lax.ppermute only.
A program may use at most 128 MiB of HBM per device.

v0:
```python
import math
import jax
import jax.numpy as jnp
from jax import lax
from jax.sharding import PartitionSpec as P

MB = 64
precise = lax.Precision.HIGHEST
coefficient = 0.044715
root_scale = math.sqrt(2.0 / math.pi)


def shortened(x):
    return jax.tree.map(lambda a: a.astype(jnp.bfloat16) if a.dtype == jnp.float32 else a, x)


def shifted(block, axis, distance):
    devices = range(lax.axis_size(axis))
    route = [(i - distance, i) for i in devices if i - distance in devices]
    return lax.ppermute(block, axis, route)


def gelu_pair(z_value):
    tanh_part = jnp.tanh(root_scale * (z_value + coefficient * z_value * z_value * z_value))
    result = 0.5 * z_value * (1.0 + tanh_part)
    derivative = 0.5 * (1.0 + tanh_part) + 0.5 * z_value * (
        1.0 - tanh_part * tanh_part
    ) * root_scale * (1.0 + 3.0 * coefficient * z_value * z_value)
    return (result, derivative)


def minibatch(carried, inputs):
    pair, bias_hidden, bias_out = carried
    queries, key_rows, values, step_rate = inputs
    w_first = pair[0]
    w_second = pair[1]
    block_len = queries.shape[1]
    causal = jnp.tril(jnp.ones((block_len, block_len), dtype=bool))
    z_first = (
        jnp.einsum("hbd,hdf->hbf", key_rows, w_first, precision=precise) + bias_hidden[:, None, :]
    )
    hidden, derivative = gelu_pair(z_first)
    z_second = (
        jnp.einsum("hbf,hdf->hbd", hidden, w_second, precision=precise) + bias_out[:, None, :]
    )
    grad_second = z_second - (values - key_rows)
    grad_first = jnp.einsum("hbd,hdf->hbf", grad_second, w_second, precision=precise) * derivative
    scores_first = jnp.einsum("htd,hsd->hts", queries, key_rows, precision=precise) + 1.0
    mix_first = jnp.where(causal[None], scores_first * step_rate[:, None, :], 0.0)
    zq_first = (
        jnp.einsum("htd,hdf->htf", queries, w_first, precision=precise) + bias_hidden[:, None, :]
    )
    zq_first = zq_first - jnp.einsum("hts,hsf->htf", mix_first, grad_first, precision=precise)
    hidden_query, unused = gelu_pair(zq_first)
    scores_second = jnp.einsum("htf,hsf->hts", hidden_query, hidden, precision=precise) + 1.0
    mix_second = jnp.where(causal[None], scores_second * step_rate[:, None, :], 0.0)
    zq_second = (
        jnp.einsum("htf,hdf->htd", hidden_query, w_second, precision=precise) + bias_out[:, None, :]
    )
    zq_second = zq_second - jnp.einsum("hts,hsd->htd", mix_second, grad_second, precision=precise)
    scaled_first = grad_first * step_rate[:, :, None]
    scaled_second = grad_second * step_rate[:, :, None]
    new_first = w_first - jnp.einsum("hbd,hbf->hdf", key_rows, scaled_first, precision=precise)
    new_second = w_second - jnp.einsum("hbd,hbf->hdf", scaled_second, hidden, precision=precise)
    new_pair = jnp.stack([new_first, new_second])
    new_hidden = bias_hidden - jnp.sum(scaled_first, axis=1)
    new_out = bias_out - jnp.sum(scaled_second, axis=1)
    return ((new_pair, new_hidden, new_out), queries + zq_second)


def run_slab(start_state, column_block, rate_block, gain_rows):
    slab_len = column_block.shape[0]
    group_heads = column_block.shape[2]
    head_size = column_block.shape[3]
    batches = slab_len // MB
    inputs = (
        column_block.astype(jnp.float32)
        .reshape(batches, MB, 3, group_heads, head_size)
        .transpose(2, 0, 3, 1, 4)
    )
    step_rate = rate_block.reshape(batches, MB, group_heads).transpose(0, 2, 1)
    final_state, results = lax.scan(
        minibatch, start_state, (inputs[0], inputs[1], inputs[2], step_rate)
    )
    results = results.transpose(0, 2, 1, 3).reshape(slab_len, group_heads, head_size)
    normed = (
        results * lax.rsqrt(jnp.mean(results * results, axis=-1, keepdims=True) + 1e-06) * gain_rows
    )
    return (final_state, normed.reshape(slab_len, group_heads * head_size).astype(jnp.bfloat16))


def on_device(
    frames,
    proj_weight,
    rate_weight,
    rate_bias,
    init_weights,
    init_bias_hidden,
    init_bias_out,
    out_gain,
):
    clip_count, slab_len, model_width = frames.shape
    head_count = rate_weight.shape[1]
    head_size = init_weights.shape[2]
    inner_width = init_weights.shape[3]
    token_rows = frames.reshape(clip_count * slab_len, model_width)
    full_weight = lax.all_gather(proj_weight, "dp", axis=0, tiled=True)
    projected = jnp.dot(token_rows, full_weight, preferred_element_type=jnp.float32)
    projected = projected.astype(jnp.bfloat16).reshape(
        clip_count, slab_len, 3, head_count, head_size
    )
    rates = jax.nn.sigmoid(
        jnp.dot(token_rows, rate_weight, preferred_element_type=jnp.float32) + rate_bias
    ) / (MB * (head_size + inner_width))
    rates = rates.reshape(clip_count, slab_len, head_count)
    gain_all = out_gain.reshape(head_count, head_size)
    length = lax.axis_size("seq")
    position = lax.axis_index("seq")
    turns = clip_count + length - 1
    received_start = (
        jnp.zeros((2, head_count, head_size, inner_width), jnp.bfloat16),
        jnp.zeros((head_count, inner_width), jnp.bfloat16),
        jnp.zeros((head_count, head_size), jnp.bfloat16),
    )
    outputs_start = jnp.zeros((clip_count, slab_len, head_count * head_size), jnp.bfloat16)
    own_state = (init_weights, init_bias_hidden, init_bias_out)

    def one_turn(turn_index, carry):
        received, outputs = carry
        unit_index = turn_index - position
        active = (unit_index >= 0) & (unit_index < clip_count)
        clip_index = jnp.clip(unit_index, 0, clip_count - 1)
        start_state = jax.tree.map(
            lambda member, other: jnp.where(position == 0, member, other.astype(jnp.float32)),
            own_state,
            received,
        )

        def run_unit(operands):
            entry_state, current = operands
            clip_block = lax.dynamic_index_in_dim(projected, clip_index, 0, keepdims=False)
            rate_block = lax.dynamic_index_in_dim(rates, clip_index, 0, keepdims=False)
            final_state, result = run_slab(entry_state, clip_block, rate_block, gain_all)
            current = lax.dynamic_update_slice(
                current, result[None], (clip_index, jnp.int32(0), jnp.int32(0))
            )
            return (jax.tree.map(lambda member: member.astype(jnp.bfloat16), final_state), current)

        def pass_through(operands):
            entry_state, current = operands
            return (jax.tree.map(lambda member: member.astype(jnp.bfloat16), entry_state), current)

        sent, outputs = lax.cond(active, run_unit, pass_through, (start_state, outputs))
        received = jax.tree.map(
            lambda part, own: part.astype(own.dtype), shifted(shortened(sent), "seq", 1), sent
        )
        return (received, outputs)

    unused, outputs = lax.fori_loop(0, turns, one_turn, (received_start, outputs_start))
    return outputs


def solution(mesh):
    return jax.shard_map(
        on_device,
        mesh=mesh,
        in_specs=(P("dp", "seq", None), P("dp", None), P(), P(), P(), P(), P(), P()),
        out_specs=P("dp", "seq", None),
        check_vma=False,
    )
```

profile of v0, /device:TPU:30, one launch (start us, length us, event | category | flops | bytes accessed | tf_op | source)
XLA Modules:
  0.0 1591.7 jit_solution(12472045964157043991)
XLA Ops:
  9.4 160.1 %all-gather.2.cloned.1.call-done = bf16[3072,4608]{1,0:T(8,128)(2,1)} async-done(((bf16[96,4608]{1,0:T(8,128)(2,1)}), bf16[3072,4608]{1,0:T(8,128)(2,1)}) %all-gather.2.cloned.1.call-update) | async-done | bytes 28311568 | tf_op jit(solution)/shard_map/all_gather | solution.py:107
  169.5 14.4 convolution_convert_fusion
  183.9 6.9 reshape.105
  190.9 6.4 copy.44
  199.6 1382.8 %while.36 = (s32[]{:T(128)}, bf16[2,24,64,256]{3,2,1,0:T(8,128)(2,1)}, bf16[24,256]{1,0:T(8,128)(2,1)S(1)}, bf16[24,64]{1,0:T(8,128)(2,1)S(1)}, bf16[2,128,1536]...) while((s32[]{:T(128)}, ...), condition=%wide.region_8.9_spmd, body=%wide.region_0.8_spmd.sunk | while | flops 2897933824 | bytes 141774256 | solution.py:159
  207.1 36.6 %collective-permute-done.2 = bf16[24,64]{1,0:T(8,128)(2,1)S(1)} collective-permute-done((bf16[24,64]{1,0:T(8,128)(2,1)S(1)}, bf16[24,64]{1,0:T(8,128)(2,1)S(1)}, u32[]{:S(2)}, u32[]{:S(2)}) %collective-permute-start.2) | collective-permute-done | bytes 3104 | tf_op jit(solution)/shard_map/while/body/eval_jaxpr/ppermute | solution.py:20
  252.2 35.8 %collective-permute-done.2 = bf16[24,64]{1,0:T(8,128)(2,1)S(1)} collective-permute-done((bf16[24,64]{1,0:T(8,128)(2,1)S(1)}, bf16[24,64]{1,0:T(8,128)(2,1)S(1)}, u32[]{:S(2)}, u32[]{:S(2)}) %collective-permute-start.2) | collective-permute-done | bytes 3104 | tf_op jit(solution)/shard_map/while/body/eval_jaxpr/ppermute | solution.py:20
  296.4 34.9 %collective-permute-done.2 = bf16[24,64]{1,0:T(8,128)(2,1)S(1)} collective-permute-done((bf16[24,64]{1,0:T(8,128)(2,1)S(1)}, bf16[24,64]{1,0:T(8,128)(2,1)S(1)}, u32[]{:S(2)}, u32[]{:S(2)}) %collective-permute-start.2) | collective-permute-done | bytes 3104 | tf_op jit(solution)/shard_map/while/body/eval_jaxpr/ppermute | solution.py:20
  339.7 34.8 %collective-permute-done.2 = bf16[24,64]{1,0:T(8,128)(2,1)S(1)} collective-permute-done((bf16[24,64]{1,0:T(8,128)(2,1)S(1)}, bf16[24,64]{1,0:T(8,128)(2,1)S(1)}, u32[]{:S(2)}, u32[]{:S(2)}) %collective-permute-start.2) | collective-permute-done | bytes 3104 | tf_op jit(solution)/shard_map/while/body/eval_jaxpr/ppermute | solution.py:20
  382.9 33.9 %collective-permute-done.2 = bf16[24,64]{1,0:T(8,128)(2,1)S(1)} collective-permute-done((bf16[24,64]{1,0:T(8,128)(2,1)S(1)}, bf16[24,64]{1,0:T(8,128)(2,1)S(1)}, u32[]{:S(2)}, u32[]{:S(2)}) %collective-permute-start.2) | collective-permute-done | bytes 3104 | tf_op jit(solution)/shard_map/while/body/eval_jaxpr/ppermute | solution.py:20
  425.3 33.0 %collective-permute-done.2 = bf16[24,64]{1,0:T(8,128)(2,1)S(1)} collective-permute-done((bf16[24,64]{1,0:T(8,128)(2,1)S(1)}, bf16[24,64]{1,0:T(8,128)(2,1)S(1)}, u32[]{:S(2)}, u32[]{:S(2)}) %collective-permute-start.2) | collective-permute-done | bytes 3104 | tf_op jit(solution)/shard_map/while/body/eval_jaxpr/ppermute | solution.py:20
  466.7 809.2 %collective-permute-done.2 = bf16[24,64]{1,0:T(8,128)(2,1)S(1)} collective-permute-done((bf16[24,64]{1,0:T(8,128)(2,1)S(1)}, bf16[24,64]{1,0:T(8,128)(2,1)S(1)}, u32[]{:S(2)}, u32[]{:S(2)}) %collective-permute-start.2) | collective-permute-done | bytes 3104 | tf_op jit(solution)/shard_map/while/body/eval_jaxpr/ppermute | solution.py:20
  1279.0 112.1 %conditional.2 = ((bf16[2,128,1536]{1,2,0:T(8,128)(2,1)}, f32[2,24,64,256]{3,2,1,0:T(8,128)S(1)}, f32[24,256]{1,0:T(8,128)S(1)}, f32[24,64]{1,0:T(8,128)S(1)})) conditional(s32[]{:T(128)} %convert_element_type.81, (bf16[2,128,1536]{1,2,0:T(8,128)(2,1)}, f32[2,24,64,256]{3,2,1,0:T(8,128)S(1)}, f32[24,256]{1,0:T(8,128)S(1)}, ...), branch_computations={%region_1.1_spmd, %region_2.7_spmd} | conditional | flops 2895551488 | bytes 116423672 | solution.py:153
  1282.1 5.8 reshape.104
  1287.9 3.8 slice_bitcast_fusion
  1291.8 88.4 %while.35 = (s32[]{:T(128)}, f32[2,24,64,256]{3,2,1,0:T(8,128)S(1)}, f32[24,256]{1,0:T(8,128)S(1)}, f32[24,64]{1,0:T(8,128)S(1)}, f32[2,24,64,64]{3,2,1,0:T(8,12...) while((s32[]{:T(128)}, ...), condition=%wide.region_6.5_spmd, body=%wide.region_3.4_spmd.sunk | while | flops 2893975552 | bytes 98181968 | solution.py:82
  1306.6 4.1 multiply_reduce_fusion.5
  1331.1 4.5 fusion.140
  1350.8 4.1 multiply_reduce_fusion.5
  1375.3 4.5 fusion.140
  1380.2 3.7 copy.41
  1396.4 33.0 %collective-permute-done.2 = bf16[24,64]{1,0:T(8,128)(2,1)S(1)} collective-permute-done((bf16[24,64]{1,0:T(8,128)(2,1)S(1)}, bf16[24,64]{1,0:T(8,128)(2,1)S(1)}, u32[]{:S(2)}, u32[]{:S(2)}) %collective-permute-start.2) | collective-permute-done | bytes 3104 | tf_op jit(solution)/shard_map/while/body/eval_jaxpr/ppermute | solution.py:20
  1432.5 112.1 %conditional.2 = ((bf16[2,128,1536]{1,2,0:T(8,128)(2,1)}, f32[2,24,64,256]{3,2,1,0:T(8,128)S(1)}, f32[24,256]{1,0:T(8,128)S(1)}, f32[24,64]{1,0:T(8,128)S(1)})) conditional(s32[]{:T(128)} %convert_element_type.81, (bf16[2,128,1536]{1,2,0:T(8,128)(2,1)}, f32[2,24,64,256]{3,2,1,0:T(8,128)S(1)}, f32[24,256]{1,0:T(8,128)S(1)}, ...), branch_computations={%region_1.1_spmd, %region_2.7_spmd} | conditional | flops 2895551488 | bytes 116423672 | solution.py:153
  1435.6 5.8 reshape.104
  1441.4 3.8 slice_bitcast_fusion
  1445.3 88.4 %while.35 = (s32[]{:T(128)}, f32[2,24,64,256]{3,2,1,0:T(8,128)S(1)}, f32[24,256]{1,0:T(8,128)S(1)}, f32[24,64]{1,0:T(8,128)S(1)}, f32[2,24,64,64]{3,2,1,0:T(8,12...) while((s32[]{:T(128)}, ...), condition=%wide.region_6.5_spmd, body=%wide.region_3.4_spmd.sunk | while | flops 2893975552 | bytes 98181968 | solution.py:82
  1460.0 4.1 multiply_reduce_fusion.5
  1484.6 4.5 fusion.140
  1504.2 4.1 multiply_reduce_fusion.5
  1528.8 4.5 fusion.140
  1533.7 3.7 copy.41
  1549.9 31.4 %collective-permute-done.2 = bf16[24,64]{1,0:T(8,128)(2,1)S(1)} collective-permute-done((bf16[24,64]{1,0:T(8,128)(2,1)S(1)}, bf16[24,64]{1,0:T(8,128)(2,1)S(1)}, u32[]{:S(2)}, u32[]{:S(2)}) %collective-permute-start.2) | collective-permute-done | bytes 3104 | tf_op jit(solution)/shard_map/while/body/eval_jaxpr/ppermute | solution.py:20
  (307 shorter events, 245.1 us)
Async XLA Ops:
  6.5 163.0 %all-gather.2.cloned.1.call-start = ((), (), s32[]{:S(2)}) async-start(), calls=%async_computation | async-start | bytes 29196288 | tf_op jit(solution)/shard_map/all_gather | solution.py:107
  203.2 40.5 %collective-permute-start = (bf16[2,24,64,256]{3,2,1,0:T(8,128)(2,1)}, bf16[2,24,64,256]{3,2,1,0:T(8,128)(2,1)S(1)}, u32[]{:S(2)}, u32[]{:S(2)}) collective-permute-start(bf16[2,24,64,256]{3,2,1,0:T(8,128)(2,1)} %convert_element_type.82), channel_id=1, source_target_pairs={{0,32},{32,64},{64,96},{96,128},{128,160},{160,192},{192,224},{1,3... | collective-permute-start | bytes 4718600 | tf_op jit(solution)/shard_map/while/body/eval_jaxpr/ppermute | solution.py:20
  204.5 39.2 %collective-permute-start.1 = (bf16[24,256]{1,0:T(8,128)(2,1)S(1)}, bf16[24,256]{1,0:T(8,128)(2,1)S(1)}, u32[]{:S(2)}, u32[]{:S(2)}) collective-permute-start(bf16[24,256]{1,0:T(8,128)(2,1)S(1)} %convert_element_type.83), channel_id=1, source_target_pairs={{0,32},{32,64},{64,96},{96,128},{128,160},{160,192},{192,224},{1,3... | collective-permute-start | bytes 36872 | tf_op jit(solution)/shard_map/while/body/eval_jaxpr/ppermute | solution.py:20
  205.8 37.9 %collective-permute-start.2 = (bf16[24,64]{1,0:T(8,128)(2,1)S(1)}, bf16[24,64]{1,0:T(8,128)(2,1)S(1)}, u32[]{:S(2)}, u32[]{:S(2)}) collective-permute-start(bf16[24,64]{1,0:T(8,128)(2,1)S(1)} %convert_element_type.84), channel_id=1, source_target_pairs={{0,32},{32,64},{64,96},{96,128},{128,160},{160,192},{192,224},{1,3... | collective-permute-start | bytes 9224 | tf_op jit(solution)/shard_map/while/body/eval_jaxpr/ppermute | solution.py:20
  248.2 39.7 %collective-permute-start = (bf16[2,24,64,256]{3,2,1,0:T(8,128)(2,1)}, bf16[2,24,64,256]{3,2,1,0:T(8,128)(2,1)S(1)}, u32[]{:S(2)}, u32[]{:S(2)}) collective-permute-start(bf16[2,24,64,256]{3,2,1,0:T(8,128)(2,1)} %convert_element_type.82), channel_id=1, source_target_pairs={{0,32},{32,64},{64,96},{96,128},{128,160},{160,192},{192,224},{1,3... | collective-permute-start | bytes 4718600 | tf_op jit(solution)/shard_map/while/body/eval_jaxpr/ppermute | solution.py:20
  249.5 38.4 %collective-permute-start.1 = (bf16[24,256]{1,0:T(8,128)(2,1)S(1)}, bf16[24,256]{1,0:T(8,128)(2,1)S(1)}, u32[]{:S(2)}, u32[]{:S(2)}) collective-permute-start(bf16[24,256]{1,0:T(8,128)(2,1)S(1)} %convert_element_type.83), channel_id=1, source_target_pairs={{0,32},{32,64},{64,96},{96,128},{128,160},{160,192},{192,224},{1,3... | collective-permute-start | bytes 36872 | tf_op jit(solution)/shard_map/while/body/eval_jaxpr/ppermute | solution.py:20
  250.8 37.1 %collective-permute-start.2 = (bf16[24,64]{1,0:T(8,128)(2,1)S(1)}, bf16[24,64]{1,0:T(8,128)(2,1)S(1)}, u32[]{:S(2)}, u32[]{:S(2)}) collective-permute-start(bf16[24,64]{1,0:T(8,128)(2,1)S(1)} %convert_element_type.84), channel_id=1, source_target_pairs={{0,32},{32,64},{64,96},{96,128},{128,160},{160,192},{192,224},{1,3... | collective-permute-start | bytes 9224 | tf_op jit(solution)/shard_map/while/body/eval_jaxpr/ppermute | solution.py:20
  292.5 38.8 %collective-permute-start = (bf16[2,24,64,256]{3,2,1,0:T(8,128)(2,1)}, bf16[2,24,64,256]{3,2,1,0:T(8,128)(2,1)S(1)}, u32[]{:S(2)}, u32[]{:S(2)}) collective-permute-start(bf16[2,24,64,256]{3,2,1,0:T(8,128)(2,1)} %convert_element_type.82), channel_id=1, source_target_pairs={{0,32},{32,64},{64,96},{96,128},{128,160},{160,192},{192,224},{1,3... | collective-permute-start | bytes 4718600 | tf_op jit(solution)/shard_map/while/body/eval_jaxpr/ppermute | solution.py:20
  293.8 37.5 %collective-permute-start.1 = (bf16[24,256]{1,0:T(8,128)(2,1)S(1)}, bf16[24,256]{1,0:T(8,128)(2,1)S(1)}, u32[]{:S(2)}, u32[]{:S(2)}) collective-permute-start(bf16[24,256]{1,0:T(8,128)(2,1)S(1)} %convert_element_type.83), channel_id=1, source_target_pairs={{0,32},{32,64},{64,96},{96,128},{128,160},{160,192},{192,224},{1,3... | collective-permute-start | bytes 36872 | tf_op jit(solution)/shard_map/while/body/eval_jaxpr/ppermute | solution.py:20
  295.1 36.2 %collective-permute-start.2 = (bf16[24,64]{1,0:T(8,128)(2,1)S(1)}, bf16[24,64]{1,0:T(8,128)(2,1)S(1)}, u32[]{:S(2)}, u32[]{:S(2)}) collective-permute-start(bf16[24,64]{1,0:T(8,128)(2,1)S(1)} %convert_element_type.84), channel_id=1, source_target_pairs={{0,32},{32,64},{64,96},{96,128},{128,160},{160,192},{192,224},{1,3... | collective-permute-start | bytes 9224 | tf_op jit(solution)/shard_map/while/body/eval_jaxpr/ppermute | solution.py:20
  335.8 38.8 %collective-permute-start = (bf16[2,24,64,256]{3,2,1,0:T(8,128)(2,1)}, bf16[2,24,64,256]{3,2,1,0:T(8,128)(2,1)S(1)}, u32[]{:S(2)}, u32[]{:S(2)}) collective-permute-start(bf16[2,24,64,256]{3,2,1,0:T(8,128)(2,1)} %convert_element_type.82), channel_id=1, source_target_pairs={{0,32},{32,64},{64,96},{96,128},{128,160},{160,192},{192,224},{1,3... | collective-permute-start | bytes 4718600 | tf_op jit(solution)/shard_map/while/body/eval_jaxpr/ppermute | solution.py:20
  337.1 37.4 %collective-permute-start.1 = (bf16[24,256]{1,0:T(8,128)(2,1)S(1)}, bf16[24,256]{1,0:T(8,128)(2,1)S(1)}, u32[]{:S(2)}, u32[]{:S(2)}) collective-permute-start(bf16[24,256]{1,0:T(8,128)(2,1)S(1)} %convert_element_type.83), channel_id=1, source_target_pairs={{0,32},{32,64},{64,96},{96,128},{128,160},{160,192},{192,224},{1,3... | collective-permute-start | bytes 36872 | tf_op jit(solution)/shard_map/while/body/eval_jaxpr/ppermute | solution.py:20
  338.4 36.1 %collective-permute-start.2 = (bf16[24,64]{1,0:T(8,128)(2,1)S(1)}, bf16[24,64]{1,0:T(8,128)(2,1)S(1)}, u32[]{:S(2)}, u32[]{:S(2)}) collective-permute-start(bf16[24,64]{1,0:T(8,128)(2,1)S(1)} %convert_element_type.84), channel_id=1, source_target_pairs={{0,32},{32,64},{64,96},{96,128},{128,160},{160,192},{192,224},{1,3... | collective-permute-start | bytes 9224 | tf_op jit(solution)/shard_map/while/body/eval_jaxpr/ppermute | solution.py:20
  379.0 37.9 %collective-permute-start = (bf16[2,24,64,256]{3,2,1,0:T(8,128)(2,1)}, bf16[2,24,64,256]{3,2,1,0:T(8,128)(2,1)S(1)}, u32[]{:S(2)}, u32[]{:S(2)}) collective-permute-start(bf16[2,24,64,256]{3,2,1,0:T(8,128)(2,1)} %convert_element_type.82), channel_id=1, source_target_pairs={{0,32},{32,64},{64,96},{96,128},{128,160},{160,192},{192,224},{1,3... | collective-permute-start | bytes 4718600 | tf_op jit(solution)/shard_map/while/body/eval_jaxpr/ppermute | solution.py:20
  380.3 36.6 %collective-permute-start.1 = (bf16[24,256]{1,0:T(8,128)(2,1)S(1)}, bf16[24,256]{1,0:T(8,128)(2,1)S(1)}, u32[]{:S(2)}, u32[]{:S(2)}) collective-permute-start(bf16[24,256]{1,0:T(8,128)(2,1)S(1)} %convert_element_type.83), channel_id=1, source_target_pairs={{0,32},{32,64},{64,96},{96,128},{128,160},{160,192},{192,224},{1,3... | collective-permute-start | bytes 36872 | tf_op jit(solution)/shard_map/while/body/eval_jaxpr/ppermute | solution.py:20
  381.6 35.2 %collective-permute-start.2 = (bf16[24,64]{1,0:T(8,128)(2,1)S(1)}, bf16[24,64]{1,0:T(8,128)(2,1)S(1)}, u32[]{:S(2)}, u32[]{:S(2)}) collective-permute-start(bf16[24,64]{1,0:T(8,128)(2,1)S(1)} %convert_element_type.84), channel_id=1, source_target_pairs={{0,32},{32,64},{64,96},{96,128},{128,160},{160,192},{192,224},{1,3... | collective-permute-start | bytes 9224 | tf_op jit(solution)/shard_map/while/body/eval_jaxpr/ppermute | solution.py:20
  421.4 36.9 %collective-permute-start = (bf16[2,24,64,256]{3,2,1,0:T(8,128)(2,1)}, bf16[2,24,64,256]{3,2,1,0:T(8,128)(2,1)S(1)}, u32[]{:S(2)}, u32[]{:S(2)}) collective-permute-start(bf16[2,24,64,256]{3,2,1,0:T(8,128)(2,1)} %convert_element_type.82), channel_id=1, source_target_pairs={{0,32},{32,64},{64,96},{96,128},{128,160},{160,192},{192,224},{1,3... | collective-permute-start | bytes 4718600 | tf_op jit(solution)/shard_map/while/body/eval_jaxpr/ppermute | solution.py:20
  422.7 35.6 %collective-permute-start.1 = (bf16[24,256]{1,0:T(8,128)(2,1)S(1)}, bf16[24,256]{1,0:T(8,128)(2,1)S(1)}, u32[]{:S(2)}, u32[]{:S(2)}) collective-permute-start(bf16[24,256]{1,0:T(8,128)(2,1)S(1)} %convert_element_type.83), channel_id=1, source_target_pairs={{0,32},{32,64},{64,96},{96,128},{128,160},{160,192},{192,224},{1,3... | collective-permute-start | bytes 36872 | tf_op jit(solution)/shard_map/while/body/eval_jaxpr/ppermute | solution.py:20
  424.0 34.3 %collective-permute-start.2 = (bf16[24,64]{1,0:T(8,128)(2,1)S(1)}, bf16[24,64]{1,0:T(8,128)(2,1)S(1)}, u32[]{:S(2)}, u32[]{:S(2)}) collective-permute-start(bf16[24,64]{1,0:T(8,128)(2,1)S(1)} %convert_element_type.84), channel_id=1, source_target_pairs={{0,32},{32,64},{64,96},{96,128},{128,160},{160,192},{192,224},{1,3... | collective-permute-start | bytes 9224 | tf_op jit(solution)/shard_map/while/body/eval_jaxpr/ppermute | solution.py:20
  462.8 813.1 %collective-permute-start = (bf16[2,24,64,256]{3,2,1,0:T(8,128)(2,1)}, bf16[2,24,64,256]{3,2,1,0:T(8,128)(2,1)S(1)}, u32[]{:S(2)}, u32[]{:S(2)}) collective-permute-start(bf16[2,24,64,256]{3,2,1,0:T(8,128)(2,1)} %convert_element_type.82), channel_id=1, source_target_pairs={{0,32},{32,64},{64,96},{96,128},{128,160},{160,192},{192,224},{1,3... | collective-permute-start | bytes 4718600 | tf_op jit(solution)/shard_map/while/body/eval_jaxpr/ppermute | solution.py:20
  464.1 811.8 %collective-permute-start.1 = (bf16[24,256]{1,0:T(8,128)(2,1)S(1)}, bf16[24,256]{1,0:T(8,128)(2,1)S(1)}, u32[]{:S(2)}, u32[]{:S(2)}) collective-permute-start(bf16[24,256]{1,0:T(8,128)(2,1)S(1)} %convert_element_type.83), channel_id=1, source_target_pairs={{0,32},{32,64},{64,96},{96,128},{128,160},{160,192},{192,224},{1,3... | collective-permute-start | bytes 36872 | tf_op jit(solution)/shard_map/while/body/eval_jaxpr/ppermute | solution.py:20
  465.4 810.5 %collective-permute-start.2 = (bf16[24,64]{1,0:T(8,128)(2,1)S(1)}, bf16[24,64]{1,0:T(8,128)(2,1)S(1)}, u32[]{:S(2)}, u32[]{:S(2)}) collective-permute-start(bf16[24,64]{1,0:T(8,128)(2,1)S(1)} %convert_element_type.84), channel_id=1, source_target_pairs={{0,32},{32,64},{64,96},{96,128},{128,160},{160,192},{192,224},{1,3... | collective-permute-start | bytes 9224 | tf_op jit(solution)/shard_map/while/body/eval_jaxpr/ppermute | solution.py:20
  1331.1 4.5 copy-start.5
  1375.3 4.5 copy-start.5
  1392.5 36.9 %collective-permute-start = (bf16[2,24,64,256]{3,2,1,0:T(8,128)(2,1)}, bf16[2,24,64,256]{3,2,1,0:T(8,128)(2,1)S(1)}, u32[]{:S(2)}, u32[]{:S(2)}) collective-permute-start(bf16[2,24,64,256]{3,2,1,0:T(8,128)(2,1)} %convert_element_type.82), channel_id=1, source_target_pairs={{0,32},{32,64},{64,96},{96,128},{128,160},{160,192},{192,224},{1,3... | collective-permute-start | bytes 4718600 | tf_op jit(solution)/shard_map/while/body/eval_jaxpr/ppermute | solution.py:20
  1393.8 35.6 %collective-permute-start.1 = (bf16[24,256]{1,0:T(8,128)(2,1)S(1)}, bf16[24,256]{1,0:T(8,128)(2,1)S(1)}, u32[]{:S(2)}, u32[]{:S(2)}) collective-permute-start(bf16[24,256]{1,0:T(8,128)(2,1)S(1)} %convert_element_type.83), channel_id=1, source_target_pairs={{0,32},{32,64},{64,96},{96,128},{128,160},{160,192},{192,224},{1,3... | collective-permute-start | bytes 36872 | tf_op jit(solution)/shard_map/while/body/eval_jaxpr/ppermute | solution.py:20
  1395.1 34.3 %collective-permute-start.2 = (bf16[24,64]{1,0:T(8,128)(2,1)S(1)}, bf16[24,64]{1,0:T(8,128)(2,1)S(1)}, u32[]{:S(2)}, u32[]{:S(2)}) collective-permute-start(bf16[24,64]{1,0:T(8,128)(2,1)S(1)} %convert_element_type.84), channel_id=1, source_target_pairs={{0,32},{32,64},{64,96},{96,128},{128,160},{160,192},{192,224},{1,3... | collective-permute-start | bytes 9224 | tf_op jit(solution)/shard_map/while/body/eval_jaxpr/ppermute | solution.py:20
  1484.6 4.5 copy-start.5
  1528.8 4.5 copy-start.5
  1546.0 35.3 %collective-permute-start = (bf16[2,24,64,256]{3,2,1,0:T(8,128)(2,1)}, bf16[2,24,64,256]{3,2,1,0:T(8,128)(2,1)S(1)}, u32[]{:S(2)}, u32[]{:S(2)}) collective-permute-start(bf16[2,24,64,256]{3,2,1,0:T(8,128)(2,1)} %convert_element_type.82), channel_id=1, source_target_pairs={{0,32},{32,64},{64,96},{96,128},{128,160},{160,192},{192,224},{1,3... | collective-permute-start | bytes 4718600 | tf_op jit(solution)/shard_map/while/body/eval_jaxpr/ppermute | solution.py:20
  1547.3 34.0 %collective-permute-start.1 = (bf16[24,256]{1,0:T(8,128)(2,1)S(1)}, bf16[24,256]{1,0:T(8,128)(2,1)S(1)}, u32[]{:S(2)}, u32[]{:S(2)}) collective-permute-start(bf16[24,256]{1,0:T(8,128)(2,1)S(1)} %convert_element_type.83), channel_id=1, source_target_pairs={{0,32},{32,64},{64,96},{96,128},{128,160},{160,192},{192,224},{1,3... | collective-permute-start | bytes 36872 | tf_op jit(solution)/shard_map/while/body/eval_jaxpr/ppermute | solution.py:20
  1548.6 32.7 %collective-permute-start.2 = (bf16[24,64]{1,0:T(8,128)(2,1)S(1)}, bf16[24,64]{1,0:T(8,128)(2,1)S(1)}, u32[]{:S(2)}, u32[]{:S(2)}) collective-permute-start(bf16[24,64]{1,0:T(8,128)(2,1)S(1)} %convert_element_type.84), channel_id=1, source_target_pairs={{0,32},{32,64},{64,96},{96,128},{128,160},{160,192},{192,224},{1,3... | collective-permute-start | bytes 9224 | tf_op jit(solution)/shard_map/while/body/eval_jaxpr/ppermute | solution.py:20
  (42 other events, 90.5 us)
Sparse Core Ops, SparseCore 0:
  9.2 160.2 all-gather.1
where the time goes:
time: 1590 us
  waiting for transfers between devices  1240 us (78%)
  local copies, waits for them, and re-layouts  124 us (8%)
  matrix products  122 us (8%)
  other arithmetic  52 us (3%)
  starting transfers between devices  34.8 us (2%)
    ppermute x27, waiting for transfers between devices, shifted(): return lax.ppermute(block, axis, route)  1080 us
    all_gather x1, waiting for transfers between devices, on_device(): full_weight = lax.all_gather(proj_weight, 'dp', axis=0, tiled=True)  160 us
    dynamic_slice x24, local copies, waits for them, and re-layouts, run_slab(): lax.scan(minibatch, start_state, (inputs[0], inputs[1], inputs[2], step_r...  56.4 us
    ppermute x27, starting transfers between devices, shifted(): return lax.ppermute(block, axis, route)  34.8 us
  transfers between devices with their start and end apart: 28, of which 10 were waited for; matrix products, arithmetic and copies ran while one was open for 0% of the time, Pallas kernels for 0%

commit v1 on v0

--- a/solution.py
+++ b/solution.py
@@ -104,7 +104,9 @@
     head_size = init_weights.shape[2]
     inner_width = init_weights.shape[3]
     token_rows = frames.reshape(clip_count * slab_len, model_width)
-    full_weight = lax.all_gather(proj_weight, "dp", axis=0, tiled=True)
+    full_weight = jnp.concatenate(
+        lax.all_to_all(jnp.stack([proj_weight] * lax.axis_size("dp")), "dp", 0, 0), axis=0
+    )
     projected = jnp.dot(token_rows, full_weight, preferred_element_type=jnp.float32)
     projected = projected.astype(jnp.bfloat16).reshape(
         clip_count, slab_len, 3, head_count, head_size

time: 1590 us -> 2050 us (1.29)
  the two profiles are of different devices: /device:TPU:30 before, /device:TPU:126 now
where the time goes in v1:
time: 2050 us
  waiting for transfers between devices  1700 us (83%)
  local copies, waits for them, and re-layouts  130 us (6%)
  matrix products  121 us (6%)
  other arithmetic  53.9 us (3%)
  starting transfers between devices  43.7 us (2%)
    ppermute x27, waiting for transfers between devices, shifted(): return lax.ppermute(block, axis, route)  1060 us
    all_to_all x1, waiting for transfers between devices, on_device(): lax.all_to_all(jnp.stack([proj_weight] * lax.axis_size('dp')), 'dp', 0, 0)  634 us
    dynamic_slice x24, local copies, waits for them, and re-layouts, run_slab(): lax.scan(minibatch, start_state, (inputs[0], inputs[1], inputs[2], step_r...  56.4 us
  transfers between devices with their start and end apart: 28, of which 10 were waited for; matrix products, arithmetic and copies ran while one was open for 0% of the time, Pallas kernels for 0%

profile of v1, /device:TPU:126, one launch (start us, length us, event | category | flops | bytes accessed | tf_op | source)
XLA Modules:
  0.0 2048.9 jit_solution(13671718152490009081)
XLA Ops:
  0.0 10.5 stack.8
  10.5 8.9 all-to-all-start
  20.1 633.7 %all-to-all-done = bf16[32,96,4608]{2,1,0:T(8,128)(2,1)} async-done(((bf16[32,96,4608]{2,1,0:T(8,128)(2,1)}), bf16[32,96,4608]{2,1,0:T(8,128)(2,1)}, u32[]{:S(2)}, u32[]{:S(2)}) %all-to-all-start) | async-done | bytes 28311584 | tf_op jit(solution)/shard_map/all_to_all | solution.py:108
  653.8 14.4 convolution_convert_fusion
  668.1 6.9 reshape.111
  675.1 6.4 copy.44
  683.8 1362.6 %while.36 = (s32[]{:T(128)}, bf16[2,24,64,256]{3,2,1,0:T(8,128)(2,1)}, bf16[24,256]{1,0:T(8,128)(2,1)S(1)}, bf16[24,64]{1,0:T(8,128)(2,1)S(1)}, bf16[2,128,1536]...) while((s32[]{:T(128)}, ...), condition=%wide.region_8.9_spmd, body=%wide.region_0.8_spmd.sunk | while | flops 2897933824 | bytes 141774256 | solution.py:161
  691.5 36.0 %collective-permute-done.2 = bf16[24,64]{1,0:T(8,128)(2,1)S(1)} collective-permute-done((bf16[24,64]{1,0:T(8,128)(2,1)S(1)}, bf16[24,64]{1,0:T(8,128)(2,1)S(1)}, u32[]{:S(2)}, u32[]{:S(2)}) %collective-permute-start.2) | collective-permute-done | bytes 3104 | tf_op jit(solution)/shard_map/while/body/eval_jaxpr/ppermute | solution.py:20
  736.2 35.1 %collective-permute-done.2 = bf16[24,64]{1,0:T(8,128)(2,1)S(1)} collective-permute-done((bf16[24,64]{1,0:T(8,128)(2,1)S(1)}, bf16[24,64]{1,0:T(8,128)(2,1)S(1)}, u32[]{:S(2)}, u32[]{:S(2)}) %collective-permute-start.2) | collective-permute-done | bytes 3104 | tf_op jit(solution)/shard_map/while/body/eval_jaxpr/ppermute | solution.py:20
  779.9 34.2 %collective-permute-done.2 = bf16[24,64]{1,0:T(8,128)(2,1)S(1)} collective-permute-done((bf16[24,64]{1,0:T(8,128)(2,1)S(1)}, bf16[24,64]{1,0:T(8,128)(2,1)S(1)}, u32[]{:S(2)}, u32[]{:S(2)}) %collective-permute-start.2) | collective-permute-done | bytes 3104 | tf_op jit(solution)/shard_map/while/body/eval_jaxpr/ppermute | solution.py:20
  822.8 34.0 %collective-permute-done.2 = bf16[24,64]{1,0:T(8,128)(2,1)S(1)} collective-permute-done((bf16[24,64]{1,0:T(8,128)(2,1)S(1)}, bf16[24,64]{1,0:T(8,128)(2,1)S(1)}, u32[]{:S(2)}, u32[]{:S(2)}) %collective-permute-start.2) | collective-permute-done | bytes 3104 | tf_op jit(solution)/shard_map/while/body/eval_jaxpr/ppermute | solution.py:20
  865.4 33.2 %collective-permute-done.2 = bf16[24,64]{1,0:T(8,128)(2,1)S(1)} collective-permute-done((bf16[24,64]{1,0:T(8,128)(2,1)S(1)}, bf16[24,64]{1,0:T(8,128)(2,1)S(1)}, u32[]{:S(2)}, u32[]{:S(2)}) %collective-permute-start.2) | collective-permute-done | bytes 3104 | tf_op jit(solution)/shard_map/while/body/eval_jaxpr/ppermute | solution.py:20
  907.3 32.3 %collective-permute-done.2 = bf16[24,64]{1,0:T(8,128)(2,1)S(1)} collective-permute-done((bf16[24,64]{1,0:T(8,128)(2,1)S(1)}, bf16[24,64]{1,0:T(8,128)(2,1)S(1)}, u32[]{:S(2)}, u32[]{:S(2)}) %collective-permute-start.2) | collective-permute-done | bytes 3104 | tf_op jit(solution)/shard_map/while/body/eval_jaxpr/ppermute | solution.py:20
  948.2 796.2 %collective-permute-done.2 = bf16[24,64]{1,0:T(8,128)(2,1)S(1)} collective-permute-done((bf16[24,64]{1,0:T(8,128)(2,1)S(1)}, bf16[24,64]{1,0:T(8,128)(2,1)S(1)}, u32[]{:S(2)}, u32[]{:S(2)}) %collective-permute-start.2) | collective-permute-done | bytes 3104 | tf_op jit(solution)/shard_map/while/body/eval_jaxpr/ppermute | solution.py:20
  1747.7 110.4 %conditional.2 = ((bf16[2,128,1536]{1,2,0:T(8,128)(2,1)}, f32[2,24,64,256]{3,2,1,0:T(8,128)S(1)}, f32[24,256]{1,0:T(8,128)S(1)}, f32[24,64]{1,0:T(8,128)S(1)})) conditional(s32[]{:T(128)} %convert_element_type.81, (bf16[2,128,1536]{1,2,0:T(8,128)(2,1)}, f32[2,24,64,256]{3,2,1,0:T(8,128)S(1)}, f32[24,256]{1,0:T(8,128)S(1)}, ...), branch_computations={%region_1.1_spmd, %region_2.7_spmd} | conditional | flops 2895551488 | bytes 116423672 | solution.py:155
  1750.8 5.8 reshape.110
  1756.6 3.8 slice_bitcast_fusion
  1760.5 86.7 %while.35 = (s32[]{:T(128)}, f32[2,24,64,256]{3,2,1,0:T(8,128)S(1)}, f32[24,256]{1,0:T(8,128)S(1)}, f32[24,64]{1,0:T(8,128)S(1)}, f32[2,24,64,64]{3,2,1,0:T(8,12...) while((s32[]{:T(128)}, ...), condition=%wide.region_6.5_spmd, body=%wide.region_3.4_spmd.sunk | while | flops 2893975552 | bytes 98181968 | solution.py:82
  1774.4 4.1 multiply_reduce_fusion.5
  1799.0 4.5 fusion.140
  1817.8 4.1 multiply_reduce_fusion.5
  1842.3 4.5 fusion.140
  1863.4 32.2 %collective-permute-done.2 = bf16[24,64]{1,0:T(8,128)(2,1)S(1)} collective-permute-done((bf16[24,64]{1,0:T(8,128)(2,1)S(1)}, bf16[24,64]{1,0:T(8,128)(2,1)S(1)}, u32[]{:S(2)}, u32[]{:S(2)}) %collective-permute-start.2) | collective-permute-done | bytes 3104 | tf_op jit(solution)/shard_map/while/body/eval_jaxpr/ppermute | solution.py:20
  1898.9 110.4 %conditional.2 = ((bf16[2,128,1536]{1,2,0:T(8,128)(2,1)}, f32[2,24,64,256]{3,2,1,0:T(8,128)S(1)}, f32[24,256]{1,0:T(8,128)S(1)}, f32[24,64]{1,0:T(8,128)S(1)})) conditional(s32[]{:T(128)} %convert_element_type.81, (bf16[2,128,1536]{1,2,0:T(8,128)(2,1)}, f32[2,24,64,256]{3,2,1,0:T(8,128)S(1)}, f32[24,256]{1,0:T(8,128)S(1)}, ...), branch_computations={%region_1.1_spmd, %region_2.7_spmd} | conditional | flops 2895551488 | bytes 116423672 | solution.py:155
  1902.0 5.8 reshape.110
  1907.8 3.8 slice_bitcast_fusion
  1911.7 86.7 %while.35 = (s32[]{:T(128)}, f32[2,24,64,256]{3,2,1,0:T(8,128)S(1)}, f32[24,256]{1,0:T(8,128)S(1)}, f32[24,64]{1,0:T(8,128)S(1)}, f32[2,24,64,64]{3,2,1,0:T(8,12...) while((s32[]{:T(128)}, ...), condition=%wide.region_6.5_spmd, body=%wide.region_3.4_spmd.sunk | while | flops 2893975552 | bytes 98181968 | solution.py:82
  1925.6 4.1 multiply_reduce_fusion.5
  1950.2 4.5 fusion.140
  1969.0 4.1 multiply_reduce_fusion.5
  1993.5 4.5 fusion.140
  2014.6 30.7 %collective-permute-done.2 = bf16[24,64]{1,0:T(8,128)(2,1)S(1)} collective-permute-done((bf16[24,64]{1,0:T(8,128)(2,1)S(1)}, bf16[24,64]{1,0:T(8,128)(2,1)S(1)}, u32[]{:S(2)}, u32[]{:S(2)}) %collective-permute-start.2) | collective-permute-done | bytes 3104 | tf_op jit(solution)/shard_map/while/body/eval_jaxpr/ppermute | solution.py:20
  (311 shorter events, 248.7 us)
Async XLA Ops:
  0.0 19.4 copy-start
  10.5 9.0 copy-start.14
  10.5 9.0 copy-start.15
  10.5 643.2 %all-to-all-start = ((bf16[32,96,4608]{2,1,0:T(8,128)(2,1)}), bf16[32,96,4608]{2,1,0:T(8,128)(2,1)}, u32[]{:S(2)}, u32[]{:S(2)}) async-start(bf16[32,96,4608]{2,1,0:T(8,128)(2,1)} %stack.8), calls=%async_computation | async-start | bytes 56623104 | tf_op jit(solution)/shard_map/all_to_all | solution.py:108
  687.6 39.9 %collective-permute-start = (bf16[2,24,64,256]{3,2,1,0:T(8,128)(2,1)}, bf16[2,24,64,256]{3,2,1,0:T(8,128)(2,1)S(1)}, u32[]{:S(2)}, u32[]{:S(2)}) collective-permute-start(bf16[2,24,64,256]{3,2,1,0:T(8,128)(2,1)} %convert_element_type.82), channel_id=1, source_target_pairs={{0,32},{32,64},{64,96},{96,128},{128,160},{160,192},{192,224},{1,3... | collective-permute-start | bytes 4718600 | tf_op jit(solution)/shard_map/while/body/eval_jaxpr/ppermute | solution.py:20
  688.9 38.6 %collective-permute-start.1 = (bf16[24,256]{1,0:T(8,128)(2,1)S(1)}, bf16[24,256]{1,0:T(8,128)(2,1)S(1)}, u32[]{:S(2)}, u32[]{:S(2)}) collective-permute-start(bf16[24,256]{1,0:T(8,128)(2,1)S(1)} %convert_element_type.83), channel_id=1, source_target_pairs={{0,32},{32,64},{64,96},{96,128},{128,160},{160,192},{192,224},{1,3... | collective-permute-start | bytes 36872 | tf_op jit(solution)/shard_map/while/body/eval_jaxpr/ppermute | solution.py:20
  690.2 37.3 %collective-permute-start.2 = (bf16[24,64]{1,0:T(8,128)(2,1)S(1)}, bf16[24,64]{1,0:T(8,128)(2,1)S(1)}, u32[]{:S(2)}, u32[]{:S(2)}) collective-permute-start(bf16[24,64]{1,0:T(8,128)(2,1)S(1)} %convert_element_type.84), channel_id=1, source_target_pairs={{0,32},{32,64},{64,96},{96,128},{128,160},{160,192},{192,224},{1,3... | collective-permute-start | bytes 9224 | tf_op jit(solution)/shard_map/while/body/eval_jaxpr/ppermute | solution.py:20
  732.3 39.0 %collective-permute-start = (bf16[2,24,64,256]{3,2,1,0:T(8,128)(2,1)}, bf16[2,24,64,256]{3,2,1,0:T(8,128)(2,1)S(1)}, u32[]{:S(2)}, u32[]{:S(2)}) collective-permute-start(bf16[2,24,64,256]{3,2,1,0:T(8,128)(2,1)} %convert_element_type.82), channel_id=1, source_target_pairs={{0,32},{32,64},{64,96},{96,128},{128,160},{160,192},{192,224},{1,3... | collective-permute-start | bytes 4718600 | tf_op jit(solution)/shard_map/while/body/eval_jaxpr/ppermute | solution.py:20
  733.6 37.7 %collective-permute-start.1 = (bf16[24,256]{1,0:T(8,128)(2,1)S(1)}, bf16[24,256]{1,0:T(8,128)(2,1)S(1)}, u32[]{:S(2)}, u32[]{:S(2)}) collective-permute-start(bf16[24,256]{1,0:T(8,128)(2,1)S(1)} %convert_element_type.83), channel_id=1, source_target_pairs={{0,32},{32,64},{64,96},{96,128},{128,160},{160,192},{192,224},{1,3... | collective-permute-start | bytes 36872 | tf_op jit(solution)/shard_map/while/body/eval_jaxpr/ppermute | solution.py:20
  734.9 36.4 %collective-permute-start.2 = (bf16[24,64]{1,0:T(8,128)(2,1)S(1)}, bf16[24,64]{1,0:T(8,128)(2,1)S(1)}, u32[]{:S(2)}, u32[]{:S(2)}) collective-permute-start(bf16[24,64]{1,0:T(8,128)(2,1)S(1)} %convert_element_type.84), channel_id=1, source_target_pairs={{0,32},{32,64},{64,96},{96,128},{128,160},{160,192},{192,224},{1,3... | collective-permute-start | bytes 9224 | tf_op jit(solution)/shard_map/while/body/eval_jaxpr/ppermute | solution.py:20
  776.0 38.1 %collective-permute-start = (bf16[2,24,64,256]{3,2,1,0:T(8,128)(2,1)}, bf16[2,24,64,256]{3,2,1,0:T(8,128)(2,1)S(1)}, u32[]{:S(2)}, u32[]{:S(2)}) collective-permute-start(bf16[2,24,64,256]{3,2,1,0:T(8,128)(2,1)} %convert_element_type.82), channel_id=1, source_target_pairs={{0,32},{32,64},{64,96},{96,128},{128,160},{160,192},{192,224},{1,3... | collective-permute-start | bytes 4718600 | tf_op jit(solution)/shard_map/while/body/eval_jaxpr/ppermute | solution.py:20
  777.3 36.8 %collective-permute-start.1 = (bf16[24,256]{1,0:T(8,128)(2,1)S(1)}, bf16[24,256]{1,0:T(8,128)(2,1)S(1)}, u32[]{:S(2)}, u32[]{:S(2)}) collective-permute-start(bf16[24,256]{1,0:T(8,128)(2,1)S(1)} %convert_element_type.83), channel_id=1, source_target_pairs={{0,32},{32,64},{64,96},{96,128},{128,160},{160,192},{192,224},{1,3... | collective-permute-start | bytes 36872 | tf_op jit(solution)/shard_map/while/body/eval_jaxpr/ppermute | solution.py:20
  778.6 35.5 %collective-permute-start.2 = (bf16[24,64]{1,0:T(8,128)(2,1)S(1)}, bf16[24,64]{1,0:T(8,128)(2,1)S(1)}, u32[]{:S(2)}, u32[]{:S(2)}) collective-permute-start(bf16[24,64]{1,0:T(8,128)(2,1)S(1)} %convert_element_type.84), channel_id=1, source_target_pairs={{0,32},{32,64},{64,96},{96,128},{128,160},{160,192},{192,224},{1,3... | collective-permute-start | bytes 9224 | tf_op jit(solution)/shard_map/while/body/eval_jaxpr/ppermute | solution.py:20
  818.8 37.9 %collective-permute-start = (bf16[2,24,64,256]{3,2,1,0:T(8,128)(2,1)}, bf16[2,24,64,256]{3,2,1,0:T(8,128)(2,1)S(1)}, u32[]{:S(2)}, u32[]{:S(2)}) collective-permute-start(bf16[2,24,64,256]{3,2,1,0:T(8,128)(2,1)} %convert_element_type.82), channel_id=1, source_target_pairs={{0,32},{32,64},{64,96},{96,128},{128,160},{160,192},{192,224},{1,3... | collective-permute-start | bytes 4718600 | tf_op jit(solution)/shard_map/while/body/eval_jaxpr/ppermute | solution.py:20
  820.1 36.6 %collective-permute-start.1 = (bf16[24,256]{1,0:T(8,128)(2,1)S(1)}, bf16[24,256]{1,0:T(8,128)(2,1)S(1)}, u32[]{:S(2)}, u32[]{:S(2)}) collective-permute-start(bf16[24,256]{1,0:T(8,128)(2,1)S(1)} %convert_element_type.83), channel_id=1, source_target_pairs={{0,32},{32,64},{64,96},{96,128},{128,160},{160,192},{192,224},{1,3... | collective-permute-start | bytes 36872 | tf_op jit(solution)/shard_map/while/body/eval_jaxpr/ppermute | solution.py:20
  821.5 35.3 %collective-permute-start.2 = (bf16[24,64]{1,0:T(8,128)(2,1)S(1)}, bf16[24,64]{1,0:T(8,128)(2,1)S(1)}, u32[]{:S(2)}, u32[]{:S(2)}) collective-permute-start(bf16[24,64]{1,0:T(8,128)(2,1)S(1)} %convert_element_type.84), channel_id=1, source_target_pairs={{0,32},{32,64},{64,96},{96,128},{128,160},{160,192},{192,224},{1,3... | collective-permute-start | bytes 9224 | tf_op jit(solution)/shard_map/while/body/eval_jaxpr/ppermute | solution.py:20
  861.5 37.2 %collective-permute-start = (bf16[2,24,64,256]{3,2,1,0:T(8,128)(2,1)}, bf16[2,24,64,256]{3,2,1,0:T(8,128)(2,1)S(1)}, u32[]{:S(2)}, u32[]{:S(2)}) collective-permute-start(bf16[2,24,64,256]{3,2,1,0:T(8,128)(2,1)} %convert_element_type.82), channel_id=1, source_target_pairs={{0,32},{32,64},{64,96},{96,128},{128,160},{160,192},{192,224},{1,3... | collective-permute-start | bytes 4718600 | tf_op jit(solution)/shard_map/while/body/eval_jaxpr/ppermute | solution.py:20
  862.8 35.9 %collective-permute-start.1 = (bf16[24,256]{1,0:T(8,128)(2,1)S(1)}, bf16[24,256]{1,0:T(8,128)(2,1)S(1)}, u32[]{:S(2)}, u32[]{:S(2)}) collective-permute-start(bf16[24,256]{1,0:T(8,128)(2,1)S(1)} %convert_element_type.83), channel_id=1, source_target_pairs={{0,32},{32,64},{64,96},{96,128},{128,160},{160,192},{192,224},{1,3... | collective-permute-start | bytes 36872 | tf_op jit(solution)/shard_map/while/body/eval_jaxpr/ppermute | solution.py:20
  864.1 34.6 %collective-permute-start.2 = (bf16[24,64]{1,0:T(8,128)(2,1)S(1)}, bf16[24,64]{1,0:T(8,128)(2,1)S(1)}, u32[]{:S(2)}, u32[]{:S(2)}) collective-permute-start(bf16[24,64]{1,0:T(8,128)(2,1)S(1)} %convert_element_type.84), channel_id=1, source_target_pairs={{0,32},{32,64},{64,96},{96,128},{128,160},{160,192},{192,224},{1,3... | collective-permute-start | bytes 9224 | tf_op jit(solution)/shard_map/while/body/eval_jaxpr/ppermute | solution.py:20
  903.3 36.2 %collective-permute-start = (bf16[2,24,64,256]{3,2,1,0:T(8,128)(2,1)}, bf16[2,24,64,256]{3,2,1,0:T(8,128)(2,1)S(1)}, u32[]{:S(2)}, u32[]{:S(2)}) collective-permute-start(bf16[2,24,64,256]{3,2,1,0:T(8,128)(2,1)} %convert_element_type.82), channel_id=1, source_target_pairs={{0,32},{32,64},{64,96},{96,128},{128,160},{160,192},{192,224},{1,3... | collective-permute-start | bytes 4718600 | tf_op jit(solution)/shard_map/while/body/eval_jaxpr/ppermute | solution.py:20
  904.6 34.9 %collective-permute-start.1 = (bf16[24,256]{1,0:T(8,128)(2,1)S(1)}, bf16[24,256]{1,0:T(8,128)(2,1)S(1)}, u32[]{:S(2)}, u32[]{:S(2)}) collective-permute-start(bf16[24,256]{1,0:T(8,128)(2,1)S(1)} %convert_element_type.83), channel_id=1, source_target_pairs={{0,32},{32,64},{64,96},{96,128},{128,160},{160,192},{192,224},{1,3... | collective-permute-start | bytes 36872 | tf_op jit(solution)/shard_map/while/body/eval_jaxpr/ppermute | solution.py:20
  906.0 33.6 %collective-permute-start.2 = (bf16[24,64]{1,0:T(8,128)(2,1)S(1)}, bf16[24,64]{1,0:T(8,128)(2,1)S(1)}, u32[]{:S(2)}, u32[]{:S(2)}) collective-permute-start(bf16[24,64]{1,0:T(8,128)(2,1)S(1)} %convert_element_type.84), channel_id=1, source_target_pairs={{0,32},{32,64},{64,96},{96,128},{128,160},{160,192},{192,224},{1,3... | collective-permute-start | bytes 9224 | tf_op jit(solution)/shard_map/while/body/eval_jaxpr/ppermute | solution.py:20
  944.3 800.1 %collective-permute-start = (bf16[2,24,64,256]{3,2,1,0:T(8,128)(2,1)}, bf16[2,24,64,256]{3,2,1,0:T(8,128)(2,1)S(1)}, u32[]{:S(2)}, u32[]{:S(2)}) collective-permute-start(bf16[2,24,64,256]{3,2,1,0:T(8,128)(2,1)} %convert_element_type.82), channel_id=1, source_target_pairs={{0,32},{32,64},{64,96},{96,128},{128,160},{160,192},{192,224},{1,3... | collective-permute-start | bytes 4718600 | tf_op jit(solution)/shard_map/while/body/eval_jaxpr/ppermute | solution.py:20
  945.6 798.8 %collective-permute-start.1 = (bf16[24,256]{1,0:T(8,128)(2,1)S(1)}, bf16[24,256]{1,0:T(8,128)(2,1)S(1)}, u32[]{:S(2)}, u32[]{:S(2)}) collective-permute-start(bf16[24,256]{1,0:T(8,128)(2,1)S(1)} %convert_element_type.83), channel_id=1, source_target_pairs={{0,32},{32,64},{64,96},{96,128},{128,160},{160,192},{192,224},{1,3... | collective-permute-start | bytes 36872 | tf_op jit(solution)/shard_map/while/body/eval_jaxpr/ppermute | solution.py:20
  946.9 797.5 %collective-permute-start.2 = (bf16[24,64]{1,0:T(8,128)(2,1)S(1)}, bf16[24,64]{1,0:T(8,128)(2,1)S(1)}, u32[]{:S(2)}, u32[]{:S(2)}) collective-permute-start(bf16[24,64]{1,0:T(8,128)(2,1)S(1)} %convert_element_type.84), channel_id=1, source_target_pairs={{0,32},{32,64},{64,96},{96,128},{128,160},{160,192},{192,224},{1,3... | collective-permute-start | bytes 9224 | tf_op jit(solution)/shard_map/while/body/eval_jaxpr/ppermute | solution.py:20
  1842.3 4.5 copy-start.5
  1859.5 36.1 %collective-permute-start = (bf16[2,24,64,256]{3,2,1,0:T(8,128)(2,1)}, bf16[2,24,64,256]{3,2,1,0:T(8,128)(2,1)S(1)}, u32[]{:S(2)}, u32[]{:S(2)}) collective-permute-start(bf16[2,24,64,256]{3,2,1,0:T(8,128)(2,1)} %convert_element_type.82), channel_id=1, source_target_pairs={{0,32},{32,64},{64,96},{96,128},{128,160},{160,192},{192,224},{1,3... | collective-permute-start | bytes 4718600 | tf_op jit(solution)/shard_map/while/body/eval_jaxpr/ppermute | solution.py:20
  1860.8 34.8 %collective-permute-start.1 = (bf16[24,256]{1,0:T(8,128)(2,1)S(1)}, bf16[24,256]{1,0:T(8,128)(2,1)S(1)}, u32[]{:S(2)}, u32[]{:S(2)}) collective-permute-start(bf16[24,256]{1,0:T(8,128)(2,1)S(1)} %convert_element_type.83), channel_id=1, source_target_pairs={{0,32},{32,64},{64,96},{96,128},{128,160},{160,192},{192,224},{1,3... | collective-permute-start | bytes 36872 | tf_op jit(solution)/shard_map/while/body/eval_jaxpr/ppermute | solution.py:20
  1862.1 33.5 %collective-permute-start.2 = (bf16[24,64]{1,0:T(8,128)(2,1)S(1)}, bf16[24,64]{1,0:T(8,128)(2,1)S(1)}, u32[]{:S(2)}, u32[]{:S(2)}) collective-permute-start(bf16[24,64]{1,0:T(8,128)(2,1)S(1)} %convert_element_type.84), channel_id=1, source_target_pairs={{0,32},{32,64},{64,96},{96,128},{128,160},{160,192},{192,224},{1,3... | collective-permute-start | bytes 9224 | tf_op jit(solution)/shard_map/while/body/eval_jaxpr/ppermute | solution.py:20
  2010.7 34.6 %collective-permute-start = (bf16[2,24,64,256]{3,2,1,0:T(8,128)(2,1)}, bf16[2,24,64,256]{3,2,1,0:T(8,128)(2,1)S(1)}, u32[]{:S(2)}, u32[]{:S(2)}) collective-permute-start(bf16[2,24,64,256]{3,2,1,0:T(8,128)(2,1)} %convert_element_type.82), channel_id=1, source_target_pairs={{0,32},{32,64},{64,96},{96,128},{128,160},{160,192},{192,224},{1,3... | collective-permute-start | bytes 4718600 | tf_op jit(solution)/shard_map/while/body/eval_jaxpr/ppermute | solution.py:20
  2012.0 33.3 %collective-permute-start.1 = (bf16[24,256]{1,0:T(8,128)(2,1)S(1)}, bf16[24,256]{1,0:T(8,128)(2,1)S(1)}, u32[]{:S(2)}, u32[]{:S(2)}) collective-permute-start(bf16[24,256]{1,0:T(8,128)(2,1)S(1)} %convert_element_type.83), channel_id=1, source_target_pairs={{0,32},{32,64},{64,96},{96,128},{128,160},{160,192},{192,224},{1,3... | collective-permute-start | bytes 36872 | tf_op jit(solution)/shard_map/while/body/eval_jaxpr/ppermute | solution.py:20
  2013.3 32.0 %collective-permute-start.2 = (bf16[24,64]{1,0:T(8,128)(2,1)S(1)}, bf16[24,64]{1,0:T(8,128)(2,1)S(1)}, u32[]{:S(2)}, u32[]{:S(2)}) collective-permute-start(bf16[24,64]{1,0:T(8,128)(2,1)S(1)} %convert_element_type.84), channel_id=1, source_target_pairs={{0,32},{32,64},{64,96},{96,128},{128,160},{160,192},{192,224},{1,3... | collective-permute-start | bytes 9224 | tf_op jit(solution)/shard_map/while/body/eval_jaxpr/ppermute | solution.py:20
  (44 other events, 110.3 us)
